TPU v7x, 128 devices: a whole 4x4x4 slice. The times are simulated.
128 devices in a mesh: grp: 8 (over y, core), tok: 16 (over z, x).
Axes of the slice: x: 4, y: 4, z: 4, core: 2. Of those that a mesh axis runs over, the one named last changes fastest.
Arguments:
- pre_q: bfloat16 [8192, 4096], P(('grp', 'tok')), may hold values from -64 to 64
- pre_kv: bfloat16 [8192, 2048], P(('grp', 'tok')), may hold values from -8 to 8
- pre_segment: int32 [8, 1024], P('grp'), may hold values from 0 to 3, never falling along the last dimension, each value on 1 to 512 neighbouring positions
- dec_q: bfloat16 [128, 4096], P(('grp', 'tok')), may hold values from -64 to 64
- cache: bfloat16 [128, 512, 2048], P(('grp', 'tok')), may hold values from -8 to 8
- cache_len: int32 [128], P(('grp', 'tok')), may hold values from 1 to 512, 32768 in all
- slot_request: int32 [128], replicated, may hold values from 0 to 127, each once
- resid: bfloat16 [8320, 4096], P('grp', 'tok'), may hold values from -64 to 64
- wo: bfloat16 [4096, 4096], P(None, 'tok'), may hold values from -0.5 to 0.5
- tenant: int32 [8, 1040], P('grp'), may hold values from 0 to 3, never falling along the last dimension, each value on 1 to 520 neighbouring positions
- norm_gain: float32 [4, 4096], replicated, may hold values from 0.25 to 1.75
- w_gate: bfloat16 [4096, 12288], P(None, 'tok'), may hold values from -0.09375 to 0.09375
- w_up: bfloat16 [4096, 12288], P(None, 'tok'), may hold values from -0.09375 to 0.09375
- w_down: bfloat16 [12288, 4096], P('tok'), may hold values from -0.0546875 to 0.0546875
Outputs:
- out: bfloat16 [8320, 4096], P('grp', 'tok')
All inputs are finite; a program needn't handle non-finite values. No bound on the sum of `cache_len` on one device may be relied on, other than what follows from the above.
Results may differ from a plain program's by a relative error of at most 0.011.
Values may be sent and summed in bfloat16 or wider, within the bound.
A program may use at most 128 MiB of HBM per device.

v0:
```python
import math
import jax
import jax.numpy as jnp
from jax import lax
from jax.sharding import PartitionSpec as P

D = 4096
H = 32
KVH = 8
HD = 128
epsilon = 1e-05


def laid_out(blocks, dim):
    dims = list(blocks.shape[1:])
    dims[dim] *= blocks.shape[0]
    return jnp.moveaxis(blocks, 0, dim).reshape(dims)


def piecewise(x, axis, dim, apply, out_dim):
    size, span = (lax.axis_size(axis), x.shape[dim])
    count = 2 if span % 2 == 0 else 1
    gathered, length = ([], span // count)
    for k in range(count):
        share = lax.slice_in_dim(x, k * length, (k + 1) * length, axis=dim)
        starts = jnp.arange(size) * span + k * length
        gathered.append(jax.vmap(apply)(lax.all_gather(share, axis), starts))
    return laid_out(jnp.concatenate(gathered, axis=out_dim + 1), out_dim)


def copy_for_each(x, axis):
    copies = jnp.broadcast_to(x, (lax.axis_size(axis), *x.shape))
    return lax.all_to_all(copies, axis, split_axis=0, concat_axis=0, tiled=True)


def over_copies(x, axis):
    return copy_for_each(x, axis).sum(axis=0)


def shards(
    pre_q,
    pre_kv,
    pre_segment,
    dec_q,
    cache,
    cache_len,
    slot_request,
    resid,
    wo,
    tenant,
    norm_gain,
    w_gate,
    w_up,
    w_down,
):
    group = H // KVH
    width = KVH * HD
    tok_index = lax.axis_index("tok")
    local_rows = pre_q.shape[0]
    segment = pre_segment[0]
    query_pos = tok_index * local_rows + jnp.arange(local_rows)
    query_seg = lax.dynamic_slice_in_dim(segment, tok_index * local_rows, local_rows)
    queries = pre_q.reshape(local_rows, KVH, group, HD)
    piece = lax.all_gather(pre_kv, "tok", axis=0, tiled=True)
    running = jnp.full((KVH, group, local_rows), -jnp.inf, jnp.float32)
    totals = jnp.zeros((KVH, group, local_rows), jnp.float32)
    summed = jnp.zeros((KVH, group, local_rows, HD), jnp.float32)
    count = piece.shape[0]
    keys = piece[:, :width].reshape(count, KVH, HD)
    values = piece[:, width:].reshape(count, KVH, HD)
    key_pos = jnp.arange(count)
    allowed = (key_pos[None, :] <= query_pos[:, None]) & (segment[None, :] == query_seg[:, None])
    scores = jnp.einsum(
        "qkgd,nkd->kgqn", queries, keys, preferred_element_type=jnp.float32
    ) / math.sqrt(HD)
    scores = jnp.where(allowed, scores, -jnp.inf)
    highest = jnp.max(scores, axis=-1)
    anchor = jnp.where(jnp.isfinite(highest), highest, 0.0)
    weights = jnp.exp(scores - anchor[..., None]).astype(jnp.bfloat16)
    factor = jnp.exp(running - anchor)
    totals = totals * factor + jnp.sum(weights.astype(jnp.float32), axis=-1)
    summed = summed * factor[..., None] + jnp.einsum(
        "kgqn,nkd->kgqd", weights, values, preferred_element_type=jnp.float32
    )
    running, totals, summed = (highest, totals, summed)
    prefill_out = (
        (summed / totals[..., None])
        .transpose(2, 0, 1, 3)
        .reshape(local_rows, D)
        .astype(jnp.bfloat16)
    )
    all_queries = lax.all_gather(dec_q, ("grp", "tok"), axis=0, tiled=True)
    slot = lax.axis_index(("grp", "tok"))
    request = slot_request[slot]
    query_row = lax.dynamic_slice_in_dim(all_queries, request, 1, 0).reshape(KVH, group, HD)
    positions = cache.shape[1]
    entries = cache[0].reshape(positions, 2, KVH, HD)
    slot_scores = jnp.einsum(
        "kgd,pkd->kgp", query_row, entries[:, 0], preferred_element_type=jnp.float32
    ) / math.sqrt(HD)
    visible = jnp.arange(positions) < cache_len[0]
    slot_scores = jnp.where(visible, slot_scores, -jnp.inf)
    slot_top = jnp.max(slot_scores, axis=-1, keepdims=True)
    slot_weights = jnp.exp(slot_scores - slot_top).astype(jnp.bfloat16)
    slot_total = jnp.sum(slot_weights.astype(jnp.float32), axis=-1)
    slot_mixed = jnp.einsum(
        "kgp,pkd->kgd", slot_weights, entries[:, 1], preferred_element_type=jnp.float32
    )
    decode_out = (slot_mixed / slot_total[..., None]).reshape(1, D).astype(jnp.bfloat16)
    attended = jnp.concatenate([prefill_out, decode_out], axis=0)

    def project(piece, start):
        return jnp.dot(piece, wo, preferred_element_type=jnp.float32)

    projected = piecewise(attended, "tok", 0, project, 0)
    mixed_in = (resid.astype(jnp.float32) + projected).astype(jnp.bfloat16)
    col_count = mixed_in.shape[1]
    owners = tenant[0]
    one_hot = (owners[:, None] == jnp.arange(norm_gain.shape[0])[None, :]).astype(jnp.float32)
    wide_cols = mixed_in.astype(jnp.float32)
    partial_sq = jnp.sum(wide_cols * wide_cols, axis=-1)
    square_sum = over_copies(partial_sq, "tok")
    local_gain = lax.dynamic_slice_in_dim(norm_gain, tok_index * col_count, col_count, 1)
    gains = jnp.dot(one_hot, local_gain, precision=lax.Precision.HIGHEST)
    normed_part = (wide_cols * lax.rsqrt(square_sum / D + epsilon)[:, None] * gains).astype(
        jnp.bfloat16
    )
    piece = lax.all_gather(normed_part, "tok", axis=1, tiled=True)
    gate_part = jnp.dot(piece, w_gate, preferred_element_type=jnp.float32)
    lift_part = jnp.dot(piece, w_up, preferred_element_type=jnp.float32)
    hidden = (jax.nn.silu(gate_part) * lift_part).astype(jnp.bfloat16)
    summed_cols = lax.psum_scatter(
        lax.dot_general(
            w_down, hidden, (((0,), (1,)), ((), ())), preferred_element_type=jnp.float32
        ).astype(jnp.bfloat16),
        "tok",
        scatter_dimension=0,
        tiled=True,
    ).astype(jnp.float32)
    result = mixed_in.astype(jnp.float32) + summed_cols.T
    return result.astype(jnp.bfloat16)


def solution(mesh):
    in_specs = (
        P(("grp", "tok"), None),
        P(("grp", "tok"), None),
        P("grp", None),
        P(("grp", "tok"), None),
        P(("grp", "tok"), None, None),
        P(("grp", "tok")),
        P(),
        P("grp", "tok"),
        P(None, "tok"),
        P("grp", None),
        P(),
        P(None, "tok"),
        P(None, "tok"),
        P("tok", None),
    )
    out_specs = P("grp", "tok")
    return jax.shard_map(shards, mesh=mesh, in_specs=in_specs, out_specs=out_specs, check_vma=False)
```

profile of v0, /device:TPU:1, one launch (start us, length us, event | category | flops | bytes accessed | tf_op | source)
XLA Modules:
  0.0 468.5 jit_solution(10560985726428544450)
XLA Ops:
  6.5 0.0 copy-start
  6.5 0.0 all-gather.12.cloned.1.call-start
  6.5 0.7 all-gather.12.cloned.1.call-update
  7.3 0.0 all-gather.8.cloned.1.call-start
  7.3 0.7 all-gather.8.cloned.1.call-update
  8.0 0.0 all-gather.14.cloned.1.call-start
  8.1 1.2 dynamic_slice.13
  11.3 1.4 reshape.65
  12.7 4.0 copy.48
  17.3 0.0 copy-done.4
  17.3 0.1 fusion.29
  17.4 0.1 fusion.22
  17.5 61.7 %all-gather.12.cloned.1.call-done = bf16[128,1,4096]{2,1,0:T(2,128)(2,1)} async-done(((bf16[1,1,4096]{2,1,0:T(2,128)(2,1)}), bf16[128,1,4096]{2,1,0:T(2,128)(2,1)}) %all-gather.12.cloned.1.call-update) | async-done | bytes 1048592 | tf_op jit(solution)/shard_map/all_gather | solution.py:92
  79.3 0.8 dynamic-slice_reduce_fusion
  80.0 1.6 convert_reduce_fusion.1
  81.7 1.6 fusion.16
  83.3 46.8 %all-gather.8.cloned.1.call-done = bf16[1024,2048]{1,0:T(8,128)(2,1)} async-done(((bf16[64,2048]{1,0:T(8,128)(2,1)}), bf16[1024,2048]{1,0:T(8,128)(2,1)}) %all-gather.8.cloned.1.call-update) | async-done | bytes 4194320 | tf_op jit(solution)/shard_map/all_gather | solution.py:64
  130.1 4.7 fusion.33
  134.8 3.9 copy.59
  138.7 3.9 copy.60
  142.7 3.2 fusion.1
  145.9 0.0 copy-start.2
  145.9 2.2 convert_reduce_fusion
  148.1 0.0 copy-done.2
  148.1 2.9 fusion.14
  150.9 0.4 copy.47
  151.3 0.4 convert_element_type.63
  151.7 0.9 maximum_bitcast_fusion
  152.6 0.0 all-gather.14.cloned.1.call-update
  152.6 75.6 %all-gather.14.cloned.1.call-done = bf16[16,65,4096]{2,1,0:T(8,128)(2,1)} async-done(((bf16[1,65,4096]{2,1,0:T(8,128)(2,1)}), bf16[16,65,4096]{2,1,0:T(8,128)(2,1)}) %all-gather.14.cloned.1.call-update) | async-done | bytes 8519696 | tf_op jit(solution)/shard_map/all_gather | solution.py:27
  228.2 5.2 %fusion.9 = f32[16,65,256]{2,1,0:T(8,128)S(1)} fusion(bf16[16,65,4096]{2,1,0:T(8,128)(2,1)} %all-gather.14.cloned.1.call-done, bf16[4096,256]{1,0:T(8,128)(2,1)S(1)} %copy-done), kind=kOutput, calls=%fused_computation.15 | convolution fusion | flops 2181038080 | bytes 11681792 | tf_op jit(solution)/shard_map/vmap()/dot_general | solution.py:113
  233.4 0.0 copy-start.3
  233.4 0.2 reshape.68
  233.6 1.3 fusion.17
  234.9 0.7 broadcast_in_dim.47
  235.6 5.0 %all-to-all-start = ((f32[16,1,1040]{2,1,0:T(1,128)}), f32[16,1,1040]{2,1,0:T(1,128)S(1)}, u32[]{:S(2)}, u32[]{:S(2)}) async-start(f32[16,1,1040]{2,1,0:T(1,128)} %broadcast_in_dim.47), calls=%async_computation | async-start | bytes 147456 | tf_op jit(solution)/shard_map/all_to_all | solution.py:33
  240.6 0.0 all-gather.10.cloned.1.call-start
  240.6 6.4 %all-to-all-done = f32[16,1,1040]{2,1,0:T(1,128)S(1)} async-done(((f32[16,1,1040]{2,1,0:T(1,128)}), f32[16,1,1040]{2,1,0:T(1,128)S(1)}, u32[]{:S(2)}, u32[]{:S(2)}) %all-to-all-start) | async-done | bytes 66592 | tf_op jit(solution)/shard_map/all_to_all | solution.py:33
  247.1 0.1 reduce_sum.42
  247.2 2.1 fusion.8
  249.3 0.0 all-gather.10.cloned.1.call-update
  249.3 0.2 reduce-scatter.2.cloned.1.call-start
  249.5 77.3 %all-gather.10.cloned.1.call-done = bf16[1040,4096]{1,0:T(8,128)(2,1)} async-done(((bf16[1040,256]{1,0:T(8,128)(2,1)}), bf16[1040,4096]{1,0:T(8,128)(2,1)}) %all-gather.10.cloned.1.call-update) | async-done | bytes 8519696 | tf_op jit(solution)/shard_map/all_gather | solution.py:128
  326.9 12.2 %fusion.34 = f32[1040,768]{1,0:T(8,128)} fusion(bf16[1040,4096]{1,0:T(8,128)(2,1)} %all-gather.10.cloned.1.call-done, bf16[4096,768]{1,0:T(8,128)(2,1)} %param.25), kind=kOutput, calls=%fused_computation.62 | convolution fusion | flops 6543114240 | bytes 18006016 | tf_op jit(solution)/shard_map/dot_general | solution.py:129
  339.1 26.3 %fusion = bf16[4096,1040]{0,1:T(8,128)(2,1)} fusion(bf16[768,4096]{1,0:T(8,128)(2,1)} %param.27, bf16[1040,4096]{1,0:T(8,128)(2,1)} %all-gather.10.cloned.1.call-done, bf16[4096,768]{1,0:T(8,128)(2,1)} %param.26, f32[1040,768]{1,0:T(8,128)} %fusion.34), kind=kOutput, calls=%fused_computation.1 | convolution fusion | flops 13095280640 | bytes 32817152 | tf_op jit(solution)/shard_map/dot_general | solution.py:133
  365.4 0.0 reduce-scatter.2.cloned.1.call-update
  365.4 94.5 %reduce-scatter.2.cloned.1.call-done = bf16[256,1040]{0,1:T(8,128)(2,1)} async-done(((bf16[4096,1040]{0,1:T(8,128)(2,1)}), bf16[256,1040]{0,1:T(8,128)(2,1)}) %reduce-scatter.2.cloned.1.call-update) | async-done | bytes 532496 | tf_op jit(solution)/shard_map/reduce_scatter | solution.py:132
  460.0 2.0 fusion.18
  (12 shorter events, 0.1 us)
Async XLA Ops:
  6.5 221.7 %copy-start = (bf16[4096,256]{1,0:T(8,128)(2,1)S(1)}, bf16[4096,256]{1,0:T(8,128)(2,1)}, u32[]{:S(2)}) copy-start(bf16[4096,256]{1,0:T(8,128)(2,1)} %param.22) | copy-start | bytes 6291460
  6.5 10.8 %copy-start.4 = (s32[1,1024]{1,0:T(1,128)S(1)}, s32[1,1024]{1,0:T(1,128)}, u32[]{:S(2)}) copy-start(s32[1,1024]{1,0:T(1,128)} %param.16) | copy-start | bytes 12292
  6.5 72.7 %all-gather.12.cloned.1.call-start = ((), (), s32[]{:S(2)}) async-start(), calls=%async_computation.5 | async-start | bytes 2113536 | tf_op jit(solution)/shard_map/all_gather | solution.py:92
  7.3 122.8 %all-gather.8.cloned.1.call-start = ((), (), s32[]{:S(2)}) async-start(), calls=%async_computation.2 | async-start | bytes 4456448 | tf_op jit(solution)/shard_map/all_gather | solution.py:64
  8.0 220.2 %all-gather.14.cloned.1.call-start = ((), (), s32[]{:S(2)}) async-start(), calls=%async_computation.6 | async-start | bytes 10027008 | tf_op jit(solution)/shard_map/all_gather | solution.py:27
  145.9 2.2 copy-start.2
  233.4 7.2 %copy-start.3 = (s32[1,1040]{1,0:T(1,128)S(1)}, s32[1,1040]{1,0:T(1,128)}, u32[]{:S(2)}) copy-start(s32[1,1040]{1,0:T(1,128)} %param.23) | copy-start | bytes 12484
  235.6 11.5 %all-to-all-start = ((f32[16,1,1040]{2,1,0:T(1,128)}), f32[16,1,1040]{2,1,0:T(1,128)S(1)}, u32[]{:S(2)}, u32[]{:S(2)}) async-start(f32[16,1,1040]{2,1,0:T(1,128)} %broadcast_in_dim.47), calls=%async_computation | async-start | bytes 147456 | tf_op jit(solution)/shard_map/all_to_all | solution.py:33
  240.6 86.3 %all-gather.10.cloned.1.call-start = ((), (), s32[]{:S(2)}) async-start(), calls=%async_computation.3 | async-start | bytes 9052160 | tf_op jit(solution)/shard_map/all_gather | solution.py:128
  249.3 210.6 %reduce-scatter.2.cloned.1.call-start = ((), (), s32[]{:S(2)}) async-start(), calls=%async_computation.4 | async-start | bytes 9052160 | tf_op jit(solution)/shard_map/reduce_scatter | solution.py:132
  365.4 96.5 %copy-start.1 = (bf16[4096,256]{1,0:T(8,128)(2,1)S(1)}, bf16[4096,256]{1,0:T(8,128)(2,1)}, u32[]{:S(2)}) copy-start(bf16[4096,256]{1,0:T(8,128)(2,1)} %param.22) | copy-start | bytes 6291460
Sparse Core Ops, SparseCore 0:
  10.3 68.8 all-gather.11
  81.4 48.6 all-gather.7
  152.7 75.4 all-gather.13
  249.4 77.3 all-gather.9
  365.5 94.3 reduce-scatter.1
where the time goes:
time: 469 us; the launch traced here: 468 us
  waiting for transfers between devices  364 us (78%)
  matrix products  55.1 us (12%)
  local copies, waits for them, and re-layouts  21.7 us (5%)
  between operations  15.9 us (3%)
  other arithmetic  6.54 us (1%)
  starting transfers between devices  5.32 us (1%)
    reduce_scatter x1, waiting for transfers between devices, shards(): lax.psum_scatter(lax.dot_general(w_down, hidden, (((0,), (1,)), ((), ()))...  94.5 us
    all_gather x1, waiting for transfers between devices, shards(): piece = lax.all_gather(normed_part, 'tok', axis=1, tiled=True)  77.3 us
    all_gather x1, waiting for transfers between devices, piecewise(): gathered.append(jax.vmap(apply)(lax.all_gather(share, axis), starts))  75.6 us
    all_gather x1, waiting for transfers between devices, shards(): all_queries = lax.all_gather(dec_q, ('grp', 'tok'), axis=0, tiled=True)  61.7 us
    all_gather x1, waiting for transfers between devices, shards(): piece = lax.all_gather(pre_kv, 'tok', axis=0, tiled=True)  46.8 us
    dot_general x1, matrix products, shards(): lax.dot_general(w_down, hidden, (((0,), (1,)), ((), ())), preferred_eleme...  26.3 us
    dot_general x1, matrix products, shards(): gate_part = jnp.dot(piece, w_gate, preferred_element_type=jnp.float32)  12.2 us
    unnamed x13, local copies, waits for them, and re-layouts  11.9 us
  transfers between devices with their start and end apart: 6, of which 6 were waited for; matrix products, arithmetic and copies ran while one was open for 2% of the time, Pallas kernels for 0%

commit v1 on v0

--- a/solution.py
+++ b/solution.py
@@ -89,7 +89,10 @@
         .reshape(local_rows, D)
         .astype(jnp.bfloat16)
     )
-    all_queries = lax.all_gather(dec_q, ("grp", "tok"), axis=0, tiled=True)
+    devices = lax.axis_size(("grp", "tok"))
+    pieces = jnp.stack([dec_q for _ in range(devices)])
+    pieces = lax.all_to_all(pieces, ("grp", "tok"), split_axis=0, concat_axis=0)
+    all_queries = jnp.concatenate(pieces, axis=0)
     slot = lax.axis_index(("grp", "tok"))
     request = slot_request[slot]
     query_row = lax.dynamic_slice_in_dim(all_queries, request, 1, 0).reshape(KVH, group, HD)

time: 469 us -> 409 us (0.87)
  waiting for transfers between devices: 364 us -> 273 us
  starting transfers between devices: 5.32 us -> 17 us
  local copies, waits for them, and re-layouts: 21.7 us -> 31 us
  other arithmetic: 6.54 us -> 15.7 us
    all_gather x1 -> x0, waiting for transfers between devices: 61.7 us -> none  [shards(): all_queries = lax.all_gather(dec_q, ('grp', 'tok'), axis=0, tiled=True)]
    all_gather x1, waiting for transfers between devices: 46.8 us -> 9.31 us  [shards(): piece = lax.all_gather(pre_kv, 'tok', axis=0, tiled=True)]
    all_to_all x0 -> x1, starting transfers between devices: none -> 11.5 us  [shards(): pieces = lax.all_to_all(pieces, ('grp', 'tok'), split_axis=0, concat_axis=0)]
    all_to_all x0 -> x1, waiting for transfers between devices: none -> 9.27 us  [shards(): pieces = lax.all_to_all(pieces, ('grp', 'tok'), split_axis=0, concat_axis=0)]
    another operation x0 -> x1, other arithmetic: none -> 8.39 us  [shards(): pieces = jnp.stack([dec_q for _ in range(devices)])]
    unnamed x13 -> x19, local copies, waits for them, and re-layouts: 11.9 us -> 17 us
  transfers between devices with their start and end apart: 6 -> 6, of which waited for: 6 -> 6; matrix products, arithmetic and copies ran while one was open for 2% -> 7% of each run, Pallas kernels for 0% -> 0%
where the time goes in v1:
time: 409 us; the launch traced here: 408 us
  waiting for transfers between devices  273 us (67%)
  matrix products  55.2 us (13%)
  local copies, waits for them, and re-layouts  31 us (8%)
  starting transfers between devices  17 us (4%)
  between operations  16 us (4%)
  other arithmetic  15.7 us (4%)
    reduce_scatter x1, waiting for transfers between devices, shards(): lax.psum_scatter(lax.dot_general(w_down, hidden, (((0,), (1,)), ((), ()))...  94.6 us
    all_gather x1, waiting for transfers between devices, shards(): piece = lax.all_gather(normed_part, 'tok', axis=1, tiled=True)  77.3 us
    all_gather x1, waiting for transfers between devices, piecewise(): gathered.append(jax.vmap(apply)(lax.all_gather(share, axis), starts))  75.1 us
    dot_general x1, matrix products, shards(): lax.dot_general(w_down, hidden, (((0,), (1,)), ((), ())), preferred_eleme...  26.4 us
    unnamed x19, local copies, waits for them, and re-layouts  17 us
    dot_general x1, matrix products, shards(): gate_part = jnp.dot(piece, w_gate, preferred_element_type=jnp.float32)  12.2 us
    all_to_all x1, starting transfers between devices, shards(): pieces = lax.all_to_all(pieces, ('grp', 'tok'), split_axis=0, concat_axis=0)  11.5 us
    all_gather x1, waiting for transfers between devices, shards(): piece = lax.all_gather(pre_kv, 'tok', axis=0, tiled=True)  9.31 us
  transfers between devices with their start and end apart: 6, of which 6 were waited for; matrix products, arithmetic and copies ran while one was open for 7% of the time, Pallas kernels for 0%

profile of v1, /device:TPU:1, one launch (start us, length us, event | category | flops | bytes accessed | tf_op | source)
XLA Modules:
  0.0 407.7 jit_solution(12820647299322338144)
XLA Ops:
  6.5 0.7 all-gather.6.cloned.1.call-update
  7.3 0.8 reduce.1
  8.0 3.4 stack.2
  11.4 0.5 broadcast.59
  12.0 8.4 %reduce.5 = bf16[128,4096]{1,0:T(8,128)(2,1)S(1)} reduce(bf16[128,1,4096]{2,1,0:T(2,128)(2,1)} %stack.2, bf16[]{:T(256)} %broadcast.59), dimensions={1}, to_apply=%stack.2.reduce_sub_computation | reduce | bytes 2097154 | tf_op jit(solution)/shard_map/stack | solution.py:93
  20.4 1.6 reshape.85
  22.0 11.5 %all-to-all-start = ((bf16[128,2,2048]{2,1,0:T(2,128)(2,1)}), bf16[128,2,2048]{2,1,0:T(2,128)(2,1)S(1)}, u32[]{:S(2)}, u32[]{:S(2)}) async-start(bf16[128,2,2048]{2,1,0:T(2,128)(2,1)} %reshape.85), calls=%async_computation | async-start | bytes 2097152 | tf_op jit(solution)/shard_map/all_to_all | solution.py:94
  33.5 0.2 all-gather.10.cloned.1.call-start
  33.7 0.7 dynamic_slice.13
  36.4 2.2 reshape.71
  38.6 3.9 copy.48
  43.3 0.1 fusion.29
  43.4 0.1 fusion.22
  43.5 9.3 %all-to-all-done = bf16[128,2,2048]{2,1,0:T(2,128)(2,1)S(1)} async-done(((bf16[128,2,2048]{2,1,0:T(2,128)(2,1)}), bf16[128,2,2048]{2,1,0:T(2,128)(2,1)S(1)}, u32[]{:S(2)}, u32[]{:S(2)}) %all-to-all-start) | async-done | bytes 1048608 | tf_op jit(solution)/shard_map/all_to_all | solution.py:94
  52.8 3.5 reshape.86
  56.2 0.8 dynamic-slice_reduce_fusion
  57.0 1.7 convert_reduce_fusion.1
  58.7 1.6 fusion.16
  60.4 9.3 %all-gather.6.cloned.1.call-done = bf16[1024,2048]{1,0:T(8,128)(2,1)} async-done(((bf16[64,2048]{1,0:T(8,128)(2,1)}), bf16[1024,2048]{1,0:T(8,128)(2,1)}) %all-gather.6.cloned.1.call-update) | async-done | bytes 4194320 | tf_op jit(solution)/shard_map/all_gather | solution.py:64
  69.7 4.6 %fusion.33 = (bf16[1024,1024]{1,0:T(8,128)(2,1)}, bf16[1024,1024]{1,0:T(8,128)(2,1)}) fusion(bf16[1024,2048]{1,0:T(8,128)(2,1)} %all-gather.6.cloned.1.call-done), kind=kLoop, calls=%fused_computation.61 | loop fusion | bytes 8388608 | tf_op jit(solution)/shard_map/slice | solution.py:69
  74.3 4.0 copy.59
  78.3 4.0 copy.60
  82.3 3.2 fusion.1
  85.5 2.2 convert_reduce_fusion
  87.7 2.9 fusion.14
  90.5 0.4 copy.47
  91.0 0.4 convert_element_type.63
  91.4 0.9 maximum_bitcast_fusion
  92.2 0.0 all-gather.10.cloned.1.call-update
  92.2 75.1 %all-gather.10.cloned.1.call-done = bf16[16,65,4096]{2,1,0:T(8,128)(2,1)} async-done(((bf16[1,65,4096]{2,1,0:T(8,128)(2,1)}), bf16[16,65,4096]{2,1,0:T(8,128)(2,1)}) %all-gather.10.cloned.1.call-update) | async-done | bytes 8519696 | tf_op jit(solution)/shard_map/all_gather | solution.py:27
  167.3 5.2 %fusion.9 = f32[16,65,256]{2,1,0:T(8,128)S(1)} fusion(bf16[16,65,4096]{2,1,0:T(8,128)(2,1)} %all-gather.10.cloned.1.call-done, bf16[4096,256]{1,0:T(8,128)(2,1)S(1)} %copy-done), kind=kOutput, calls=%fused_computation.15 | convolution fusion | flops 2181038080 | bytes 11681792 | tf_op jit(solution)/shard_map/vmap()/dot_general | solution.py:116
  172.5 0.0 copy-start.4
  172.5 0.2 reshape.74
  172.7 1.3 fusion.17
  174.0 0.7 broadcast_in_dim.47
  174.7 5.0 %all-to-all-start.1 = ((f32[16,1,1040]{2,1,0:T(1,128)}), f32[16,1,1040]{2,1,0:T(1,128)S(1)}, u32[]{:S(2)}, u32[]{:S(2)}) async-start(f32[16,1,1040]{2,1,0:T(1,128)} %broadcast_in_dim.47), calls=%async_computation.1 | async-start | bytes 147456 | tf_op jit(solution)/shard_map/all_to_all | solution.py:33
  179.7 0.0 all-gather.8.cloned.1.call-start
  179.8 6.4 %all-to-all-done.1 = f32[16,1,1040]{2,1,0:T(1,128)S(1)} async-done(((f32[16,1,1040]{2,1,0:T(1,128)}), f32[16,1,1040]{2,1,0:T(1,128)S(1)}, u32[]{:S(2)}, u32[]{:S(2)}) %all-to-all-start.1) | async-done | bytes 66592 | tf_op jit(solution)/shard_map/all_to_all | solution.py:33
  186.2 0.1 reduce_sum.42
  186.3 2.1 fusion.8
  188.4 0.0 all-gather.8.cloned.1.call-update
  188.4 0.3 reduce-scatter.2.cloned.1.call-start
  188.7 77.3 %all-gather.8.cloned.1.call-done = bf16[1040,4096]{1,0:T(8,128)(2,1)} async-done(((bf16[1040,256]{1,0:T(8,128)(2,1)}), bf16[1040,4096]{1,0:T(8,128)(2,1)}) %all-gather.8.cloned.1.call-update) | async-done | bytes 8519696 | tf_op jit(solution)/shard_map/all_gather | solution.py:131
  266.0 12.2 %fusion.34 = f32[1040,768]{1,0:T(8,128)} fusion(bf16[1040,4096]{1,0:T(8,128)(2,1)} %all-gather.8.cloned.1.call-done, bf16[4096,768]{1,0:T(8,128)(2,1)} %param.25), kind=kOutput, calls=%fused_computation.62 | convolution fusion | flops 6543114240 | bytes 18006016 | tf_op jit(solution)/shard_map/dot_general | solution.py:132
  278.2 26.4 %fusion = bf16[4096,1040]{0,1:T(8,128)(2,1)} fusion(bf16[768,4096]{1,0:T(8,128)(2,1)} %param.27, bf16[1040,4096]{1,0:T(8,128)(2,1)} %all-gather.8.cloned.1.call-done, bf16[4096,768]{1,0:T(8,128)(2,1)} %param.26, f32[1040,768]{1,0:T(8,128)} %fusion.34), kind=kOutput, calls=%fused_computation.1 | convolution fusion | flops 13095280640 | bytes 32817152 | tf_op jit(solution)/shard_map/dot_general | solution.py:136
  304.5 0.0 reduce-scatter.2.cloned.1.call-update
  304.5 94.6 %reduce-scatter.2.cloned.1.call-done = bf16[256,1040]{0,1:T(8,128)(2,1)} async-done(((bf16[4096,1040]{0,1:T(8,128)(2,1)}), bf16[256,1040]{0,1:T(8,128)(2,1)}) %reduce-scatter.2.cloned.1.call-update) | async-done | bytes 532496 | tf_op jit(solution)/shard_map/reduce_scatter | solution.py:135
  399.2 2.0 fusion.18
  (21 shorter events, 0.1 us)
Async XLA Ops:
  6.5 160.8 %copy-start = (bf16[4096,256]{1,0:T(8,128)(2,1)S(1)}, bf16[4096,256]{1,0:T(8,128)(2,1)}, u32[]{:S(2)}) copy-start(bf16[4096,256]{1,0:T(8,128)(2,1)} %param.22) | copy-start | bytes 6291460
  6.5 63.1 %all-gather.6.cloned.1.call-start = ((), (), s32[]{:S(2)}) async-start(), calls=%async_computation.3 | async-start | bytes 4456448 | tf_op jit(solution)/shard_map/all_gather | solution.py:64
  12.0 21.8 %copy-start.6 = (s32[128]{0:T(128)S(1)}, s32[128]{0:T(128)}, u32[]{:S(2)}) copy-start(s32[128]{0:T(128)} %param.20) | copy-start | bytes 1540
  22.0 21.3 %copy-start.5 = (s32[1,1024]{1,0:T(1,128)S(1)}, s32[1,1024]{1,0:T(1,128)}, u32[]{:S(2)}) copy-start(s32[1,1024]{1,0:T(1,128)} %param.16) | copy-start | bytes 12292
  22.0 30.8 %all-to-all-start = ((bf16[128,2,2048]{2,1,0:T(2,128)(2,1)}), bf16[128,2,2048]{2,1,0:T(2,128)(2,1)S(1)}, u32[]{:S(2)}, u32[]{:S(2)}) async-start(bf16[128,2,2048]{2,1,0:T(2,128)(2,1)} %reshape.85), calls=%async_computation | async-start | bytes 2097152 | tf_op jit(solution)/shard_map/all_to_all | solution.py:94
  33.5 133.8 %all-gather.10.cloned.1.call-start = ((), (), s32[]{:S(2)}) async-start(), calls=%async_computation.6 | async-start | bytes 10027008 | tf_op jit(solution)/shard_map/all_gather | solution.py:27
  74.3 8.0 %copy-start.3 = (bf16[64,8,4,128]{3,2,1,0:T(4,128)(2,1)S(1)}, bf16[64,8,4,128]{3,2,1,0:T(4,128)(2,1)}, u32[]{:S(2)}) copy-start(bf16[64,8,4,128]{3,2,1,0:T(4,128)(2,1)} %reshape.71) | copy-start | bytes 1572868
  85.5 2.2 copy-start.2
  172.5 7.2 %copy-start.4 = (s32[1,1040]{1,0:T(1,128)S(1)}, s32[1,1040]{1,0:T(1,128)}, u32[]{:S(2)}) copy-start(s32[1,1040]{1,0:T(1,128)} %param.23) | copy-start | bytes 12484
  174.7 11.5 %all-to-all-start.1 = ((f32[16,1,1040]{2,1,0:T(1,128)}), f32[16,1,1040]{2,1,0:T(1,128)S(1)}, u32[]{:S(2)}, u32[]{:S(2)}) async-start(f32[16,1,1040]{2,1,0:T(1,128)} %broadcast_in_dim.47), calls=%async_computation.1 | async-start | bytes 147456 | tf_op jit(solution)/shard_map/all_to_all | solution.py:33
  179.7 86.3 %all-gather.8.cloned.1.call-start = ((), (), s32[]{:S(2)}) async-start(), calls=%async_computation.4 | async-start | bytes 9052160 | tf_op jit(solution)/shard_map/all_gather | solution.py:131
  188.4 210.7 %reduce-scatter.2.cloned.1.call-start = ((), (), s32[]{:S(2)}) async-start(), calls=%async_computation.5 | async-start | bytes 9052160 | tf_op jit(solution)/shard_map/reduce_scatter | solution.py:135
  304.5 96.6 %copy-start.1 = (bf16[4096,256]{1,0:T(8,128)(2,1)S(1)}, bf16[4096,256]{1,0:T(8,128)(2,1)}, u32[]{:S(2)}) copy-start(bf16[4096,256]{1,0:T(8,128)(2,1)} %param.22) | copy-start | bytes 6291460
Sparse Core Ops, SparseCore 0:
  9.5 60.1 all-gather.5
  92.4 74.9 all-gather.9
  188.5 77.3 all-gather.7
  304.7 94.4 reduce-scatter.1
